TPU v7x, 32 devices: a whole 2x2x4 slice. The times are simulated.
32 devices in a mesh: shots: 2 (over y), lat: 4 (over z), freq: 2 (over x), sub: 2 (over core).
Axes of the slice: x: 2, y: 2, z: 4, core: 2. Of those that a mesh axis runs over, the one named last changes fastest.
Arguments:
- wavefields: float32 [4, 4, 64, 1024], P(('shots', 'freq'), None, 'lat', 'sub'), parts along dimension 0, may hold values from -6 to 6
- velocity: float32 [8, 64, 1024], P('freq', 'lat', 'sub'), may hold values from 0 to 31
- filter_table: float32 [32, 32, 9, 2], replicated, may hold values from -1 to 1
- freq_pick: int32 [2], P('freq'), may hold values from 0 to 31
- slab_order: int32 [4], replicated, may hold values from 0 to 7
Outputs:
- fields_out: float32 [4, 4, 64, 1024], P(('shots', 'freq'), None, 'lat', 'sub'), parts along dimension 0
- image: float32 [8, 64, 1024], P(('shots', 'freq'), 'lat', 'sub'), parts along dimension 0
There are 2 independent parts, one for each index of `shots`. A program takes and returns all parts, laid end to end along the dimension named above; an argument that names none is the same for every part. Nothing has to cross between parts.
All inputs are finite; a program needn't handle non-finite values.
Results may differ from a plain program's by a relative error of at most 0.0003.
Values sent between devices are 32-bit elements; how exact they have to be, the bound alone decides.
No kernel may reach another device: no remote copies, remote signals or barrier semaphores. Data moves between devices by JAX's collectives and lax.ppermute only.
A program may use at most 64 MiB of HBM per device.

v0:
```python
import jax
import jax.numpy as jnp
from jax import lax
from jax.sharding import PartitionSpec as P

KCHEB = 8
NBINS = 32
TABLE_FREQS = 32


def padded_2(cells, sides, width):
    for axis, dim in sides:
        count = lax.axis_size(axis)
        ends = count - 1
        head = lax.slice_in_dim(cells, 0, width, axis=dim)
        tail = lax.slice_in_dim(cells, cells.shape[dim] - width, cells.shape[dim], axis=dim)
        cells = jnp.concatenate(
            [
                lax.ppermute(tail, axis, [(i, (i + 1) % count) for i in range(ends)]),
                cells,
                lax.ppermute(head, axis, [((i + 1) % count, i) for i in range(ends)]),
            ],
            axis=dim,
        )
    return cells


def spread(value, axis, source):
    kept = jnp.where(lax.axis_index(axis) == source, value, 0).astype(value.dtype)
    return lax.psum(kept, axis)


def stencil(padded):
    edges = (
        padded[:, :, 2:, 1:-1]
        + padded[:, :, :-2, 1:-1]
        + padded[:, :, 1:-1, 2:]
        + padded[:, :, 1:-1, :-2]
    )
    corners = (
        padded[:, :, 2:, 2:]
        + padded[:, :, 2:, :-2]
        + padded[:, :, :-2, 2:]
        + padded[:, :, :-2, :-2]
    )
    return -0.5 * padded[:, :, 1:-1, 1:-1] + 0.25 * edges + 0.125 * corners


def combine(pair, term):
    real_part = pair[:, 0][:, None]
    imag_part = pair[:, 1][:, None]
    turned = jnp.stack([term[:, 1], -term[:, 0], -term[:, 3], term[:, 2]], axis=1)
    return real_part * term + imag_part * turned


def trim_edges(array, width):
    return array[:, :, width : array.shape[2] - width, width : array.shape[3] - width]


def propagate(fields, coefficients):
    rows_here = fields.shape[2]
    cols_here = fields.shape[3]
    padded = padded_2(fields, (("lat", 2), ("sub", 3)), KCHEB)
    row_ids = (
        lax.axis_index("lat") * rows_here
        - KCHEB
        + jnp.arange(rows_here + 2 * KCHEB, dtype=jnp.int32)
    )
    col_ids = (
        lax.axis_index("sub") * cols_here
        - KCHEB
        + jnp.arange(cols_here + 2 * KCHEB, dtype=jnp.int32)
    )
    row_inside = (row_ids >= 0) & (row_ids < rows_here * lax.axis_size("lat"))
    col_inside = (col_ids >= 0) & (col_ids < cols_here * lax.axis_size("sub"))
    inside = (row_inside[:, None] & col_inside[None, :]).astype(jnp.float32)[None, None]
    current = stencil(padded) * trim_edges(inside, 1)
    summed = combine(coefficients[:, 0], trim_edges(padded, KCHEB))
    summed = summed + combine(coefficients[:, 1], trim_edges(current, KCHEB - 1))
    previous = trim_edges(padded, 1)
    for order in range(2, KCHEB + 1):
        following = (2.0 * stencil(current) - trim_edges(previous, 1)) * trim_edges(inside, order)
        previous = trim_edges(current, 1)
        current = following
        summed = summed + combine(coefficients[:, order], trim_edges(current, KCHEB - order))
    return summed


def body(wavefields, velocity, filter_table, freq_pick, slab_order):
    highest = lax.Precision.HIGHEST
    freq_here = wavefields.shape[0]
    rows_here = wavefields.shape[2]
    cols_here = wavefields.shape[3]
    depth_count = slab_order.shape[0]
    slab_size = velocity.shape[0]
    onehot = (freq_pick[:, None] == jnp.arange(TABLE_FREQS, dtype=jnp.int32)[None, :]).astype(
        jnp.float32
    )
    selected = jnp.einsum("ft,btkc->bfkc", onehot, filter_table, precision=highest)
    selected = selected.reshape(NBINS, freq_here * (KCHEB + 1) * 2).T
    bin_grid = jnp.arange(NBINS, dtype=jnp.float32)[:, None]
    fields = wavefields
    images = []
    for depth_step in range(depth_count):
        stored_row = slab_order[depth_step]
        owner_index = stored_row // slab_size
        local_slab = lax.dynamic_index_in_dim(velocity, stored_row % slab_size, 0, keepdims=False)
        slowness = spread(local_slab, "freq", owner_index)
        weights = jnp.maximum(0.0, 1.0 - jnp.abs(slowness.reshape(1, -1) - bin_grid))
        coefficients = jnp.dot(
            selected, weights, precision=highest, preferred_element_type=jnp.float32
        )
        coefficients = coefficients.reshape(freq_here, KCHEB + 1, 2, rows_here, cols_here)
        fields = propagate(fields, coefficients)
        images.append(jnp.sum(fields[:, 0] * fields[:, 2] + fields[:, 1] * fields[:, 3], axis=0))
    image = lax.psum_scatter(jnp.stack(images), "freq", scatter_dimension=0, tiled=True)
    return (fields, image)


def solution(mesh):
    return jax.shard_map(
        body,
        mesh=mesh,
        in_specs=(
            P(("shots", "freq"), None, "lat", "sub"),
            P("freq", "lat", "sub"),
            P(),
            P("freq"),
            P(),
        ),
        out_specs=(P(("shots", "freq"), None, "lat", "sub"), P(("shots", "freq"), "lat", "sub")),
        check_vma=False,
    )
```

profile of v0, /device:TPU:0, one launch (start us, length us, event | category | flops | bytes accessed | tf_op | source)
XLA Modules:
  0.0 132.2 jit_solution(1288073521802857635)
XLA Ops:
  7.2 0.9 fusion.356
  8.2 1.4 %collective-permute-start.1 = (f32[1,4,8,512]{3,2,1,0:T(8,128)S(1)}, f32[1,4,8,512]{3,2,1,0:T(8,128)S(1)}, u32[]{:S(2)}, u32[]{:S(2)}) collective-permute-start(f32[1,4,8,512]{3,2,1,0:T(8,128)S(1)} %get-tuple-element.207), channel_id=1, source_target_pairs={{4,0},{8,4},{12,8},{5,1},{9,5},{13,9},{6,2},{10,6},{14,10},{7,3},{... | collective-permute-start | bytes 196616 | tf_op jit(solution)/shard_map/ppermute | solution.py:21
  9.6 5.6 %collective-permute-start = (f32[1,4,8,512]{3,2,1,0:T(8,128)S(1)}, f32[1,4,8,512]{3,2,1,0:T(8,128)S(1)}, u32[]{:S(2)}, u32[]{:S(2)}) collective-permute-start(f32[1,4,8,512]{3,2,1,0:T(8,128)S(1)} %get-tuple-element.208), channel_id=1, source_target_pairs={{0,4},{4,8},{8,12},{1,5},{5,9},{9,13},{2,6},{6,10},{10,14},{3,7},{... | collective-permute-start | bytes 196616 | tf_op jit(solution)/shard_map/ppermute | solution.py:19
  30.5 1.5 %collective-permute-start.2 = (f32[1,4,32,8]{3,2,1,0:T(8,128)S(1)}, f32[1,4,32,8]{3,2,1,0:T(8,128)S(1)}, u32[]{:S(2)}, u32[]{:S(2)}) collective-permute-start(f32[1,4,32,8]{3,2,1,0:T(8,128)S(1)} %get-tuple-element.96), channel_id=1, source_target_pairs={{0,1},{2,3},{4,5},{6,7},{8,9},{10,11},{12,13},{14,15},{16,17},{18,... | collective-permute-start | bytes 12296 | tf_op jit(solution)/shard_map/ppermute | solution.py:19
  32.0 1.3 collective-permute-start.3
  33.4 1.7 %collective-permute-done.3 = f32[1,4,32,8]{3,2,1,0:T(8,128)S(1)} collective-permute-done((f32[1,4,32,8]{3,2,1,0:T(8,128)S(1)}, f32[1,4,32,8]{3,2,1,0:T(8,128)S(1)}, u32[]{:S(2)}, u32[]{:S(2)}) %collective-permute-start.3) | collective-permute-done | bytes 4128 | tf_op jit(solution)/shard_map/ppermute | solution.py:21
  40.2 0.8 fusion.330
  41.3 0.8 fusion.347
  42.1 7.4 %all-reduce.3.cloned.1.call-done = (f32[16,512]{1,0:T(8,128)}, f32[16,512]{1,0:T(8,128)}, f32[16,512]{1,0:T(8,128)}, f32[16,512]{1,0:T(8,128)}) async-done(((f32[16,512]{1,0:T(8,128)}, f32[16,512]{1,0:T(8,128)}, f32[16,512]{1,0:T(8,128)}, f32[16,512]{1,0:T(8,128)}), (f32[16,512]{1,0:T(8,128)}, f32[16,512]{1,0:T(8,128)}, f32[16,512]{1,0:T(8,128)}, f32[16,512]{1,0:T(8,128)})) %all-reduce.3.cloned.1.call-update) | async-done | bytes 131088 | tf_op jit(solution)/shard_map/psum | solution.py:30
  49.4 1.8 %convolution_bitcast_fusion = f32[1,9,2,16,512]{4,1,3,2,0:T(8,128)S(1)} fusion(f32[16,512]{1,0:T(8,128)} %get-tuple-element.2, f32[9,2,32,1]{2,1,0,3:T(2,128)S(1)} %bitcast.356), kind=kOutput, calls=%fused_computation | convolution fusion | flops 57671680 | bytes 624896 | tf_op jit(solution)/shard_map/dot_general | solution.py:110
  53.6 3.4 %collective-permute-start.4 = (f32[1,4,8,512]{3,2,1,0:T(8,128)S(1)}, f32[1,4,8,512]{3,2,1,0:T(8,128)S(1)}, u32[]{:S(2)}, u32[]{:S(2)}) collective-permute-start(f32[1,4,8,512]{3,2,1,0:T(8,128)S(1)} %get-tuple-element.193), channel_id=1, source_target_pairs={{0,4},{4,8},{8,12},{1,5},{5,9},{9,13},{2,6},{6,10},{10,14},{3,7},{... | collective-permute-start | bytes 196616 | tf_op jit(solution)/shard_map/ppermute | solution.py:19
  57.0 1.5 %collective-permute-start.5 = (f32[1,4,8,512]{3,2,1,0:T(8,128)S(1)}, f32[1,4,8,512]{3,2,1,0:T(8,128)S(1)}, u32[]{:S(2)}, u32[]{:S(2)}) collective-permute-start(f32[1,4,8,512]{3,2,1,0:T(8,128)S(1)} %get-tuple-element.194), channel_id=1, source_target_pairs={{4,0},{8,4},{12,8},{5,1},{9,5},{13,9},{6,2},{10,6},{14,10},{7,3},{... | collective-permute-start | bytes 196616 | tf_op jit(solution)/shard_map/ppermute | solution.py:21
  58.5 1.0 convolution_bitcast_fusion.1
  60.0 0.7 copy-done.26
  60.7 1.0 convolution_bitcast_fusion.2
  63.0 1.0 convolution_bitcast_fusion.3
  64.9 1.3 collective-permute-start.6
  66.2 1.3 collective-permute-start.7
  67.8 1.6 %collective-permute-done.7 = f32[1,4,32,8]{3,2,1,0:T(8,128)S(1)} collective-permute-done((f32[1,4,32,8]{3,2,1,0:T(8,128)S(1)}, f32[1,4,32,8]{3,2,1,0:T(8,128)S(1)}, u32[]{:S(2)}, u32[]{:S(2)}) %collective-permute-start.7) | collective-permute-done | bytes 4128 | tf_op jit(solution)/shard_map/ppermute | solution.py:21
  75.1 4.5 %collective-permute-start.8 = (f32[1,4,8,512]{3,2,1,0:T(8,128)S(1)}, f32[1,4,8,512]{3,2,1,0:T(8,128)S(1)}, u32[]{:S(2)}, u32[]{:S(2)}) collective-permute-start(f32[1,4,8,512]{3,2,1,0:T(8,128)S(1)} %get-tuple-element.187), channel_id=1, source_target_pairs={{0,4},{4,8},{8,12},{1,5},{5,9},{9,13},{2,6},{6,10},{10,14},{3,7},{... | collective-permute-start | bytes 196616 | tf_op jit(solution)/shard_map/ppermute | solution.py:19
  79.7 1.3 collective-permute-start.9
  81.6 4.3 %collective-permute-done.9 = f32[1,4,8,512]{3,2,1,0:T(8,128)S(1)} collective-permute-done((f32[1,4,8,512]{3,2,1,0:T(8,128)S(1)}, f32[1,4,8,512]{3,2,1,0:T(8,128)S(1)}, u32[]{:S(2)}, u32[]{:S(2)}) %collective-permute-start.9) | collective-permute-done | bytes 65568 | tf_op jit(solution)/shard_map/ppermute | solution.py:21
  85.9 1.3 collective-permute-start.10
  87.2 1.5 %collective-permute-start.11 = (f32[1,4,32,8]{3,2,1,0:T(8,128)S(1)}, f32[1,4,32,8]{3,2,1,0:T(8,128)S(1)}, u32[]{:S(2)}, u32[]{:S(2)}) collective-permute-start(f32[1,4,32,8]{3,2,1,0:T(8,128)S(1)} %get-tuple-element.93), channel_id=1, source_target_pairs={{1,0},{3,2},{5,4},{7,6},{9,8},{11,10},{13,12},{15,14},{17,16},{19,... | collective-permute-start | bytes 12296 | tf_op jit(solution)/shard_map/ppermute | solution.py:21
  88.8 1.6 %collective-permute-done.11 = f32[1,4,32,8]{3,2,1,0:T(8,128)S(1)} collective-permute-done((f32[1,4,32,8]{3,2,1,0:T(8,128)S(1)}, f32[1,4,32,8]{3,2,1,0:T(8,128)S(1)}, u32[]{:S(2)}, u32[]{:S(2)}) %collective-permute-start.11) | collective-permute-done | bytes 4128 | tf_op jit(solution)/shard_map/ppermute | solution.py:21
  96.1 3.4 %collective-permute-start.12 = (f32[1,4,8,512]{3,2,1,0:T(8,128)S(1)}, f32[1,4,8,512]{3,2,1,0:T(8,128)S(1)}, u32[]{:S(2)}, u32[]{:S(2)}) collective-permute-start(f32[1,4,8,512]{3,2,1,0:T(8,128)S(1)} %get-tuple-element.181), channel_id=1, source_target_pairs={{0,4},{4,8},{8,12},{1,5},{5,9},{9,13},{2,6},{6,10},{10,14},{3,7},{... | collective-permute-start | bytes 196616 | tf_op jit(solution)/shard_map/ppermute | solution.py:19
  99.5 1.3 collective-permute-start.13
  101.4 4.3 %collective-permute-done.13 = f32[1,4,8,512]{3,2,1,0:T(8,128)S(1)} collective-permute-done((f32[1,4,8,512]{3,2,1,0:T(8,128)S(1)}, f32[1,4,8,512]{3,2,1,0:T(8,128)S(1)}, u32[]{:S(2)}, u32[]{:S(2)}) %collective-permute-start.13) | collective-permute-done | bytes 65568 | tf_op jit(solution)/shard_map/ppermute | solution.py:21
  105.7 1.3 collective-permute-start.14
  107.0 1.3 collective-permute-start.15
  108.4 1.8 %collective-permute-done.15 = f32[1,4,32,8]{3,2,1,0:T(8,128)S(1)} collective-permute-done((f32[1,4,32,8]{3,2,1,0:T(8,128)S(1)}, f32[1,4,32,8]{3,2,1,0:T(8,128)S(1)}, u32[]{:S(2)}, u32[]{:S(2)}) %collective-permute-start.15) | collective-permute-done | bytes 4128 | tf_op jit(solution)/shard_map/ppermute | solution.py:21
  116.6 8.7 %reduce-scatter.2.cloned.1.call-done = f32[2,16,512]{2,1,0:T(8,128)} async-done(((f32[4,16,512]{2,1,0:T(8,128)}), f32[2,16,512]{2,1,0:T(8,128)}) %reduce-scatter.2.cloned.1.call-update) | async-done | bytes 65552 | tf_op jit(solution)/shard_map/reduce_scatter | solution.py:116
  (261 shorter events, 32.8 us)
Async XLA Ops:
  7.2 22.4 %copy-start = (f32[32,32,9,2]{1,3,2,0:T(2,128)S(1)}, f32[32,32,9,2]{1,3,2,0:T(2,128)}, u32[]{:S(2)}) copy-start(f32[32,32,9,2]{1,3,2,0:T(2,128)} %param.7) | copy-start | bytes 221188
  7.2 42.3 %all-reduce.3.cloned.1.call-start = ((), (), s32[]{:S(2)}) async-start(), calls=%async_computation.2 | async-start | bytes 262144 | tf_op jit(solution)/shard_map/psum | solution.py:30
  7.2 8.0 %copy-start.28 = (s32[4]{0:T(128)S(1)}, s32[4]{0:T(128)}, u32[]{:S(2)}) copy-start(s32[4]{0:T(128)} %param.9) | copy-start | bytes 52
  8.2 18.0 %copy-start.24 = (f32[4,16,512]{2,1,0:T(8,128)S(1)}, f32[4,16,512]{2,1,0:T(8,128)}, u32[]{:S(2)}) copy-start(f32[4,16,512]{2,1,0:T(8,128)} %param.6) | copy-start | bytes 393220
  8.2 22.3 %collective-permute-start.1 = (f32[1,4,8,512]{3,2,1,0:T(8,128)S(1)}, f32[1,4,8,512]{3,2,1,0:T(8,128)S(1)}, u32[]{:S(2)}, u32[]{:S(2)}) collective-permute-start(f32[1,4,8,512]{3,2,1,0:T(8,128)S(1)} %get-tuple-element.207), channel_id=1, source_target_pairs={{4,0},{8,4},{12,8},{5,1},{9,5},{13,9},{6,2},{10,6},{14,10},{7,3},{... | collective-permute-start | bytes 196616 | tf_op jit(solution)/shard_map/ppermute | solution.py:21
  9.6 20.8 %collective-permute-start = (f32[1,4,8,512]{3,2,1,0:T(8,128)S(1)}, f32[1,4,8,512]{3,2,1,0:T(8,128)S(1)}, u32[]{:S(2)}, u32[]{:S(2)}) collective-permute-start(f32[1,4,8,512]{3,2,1,0:T(8,128)S(1)} %get-tuple-element.208), channel_id=1, source_target_pairs={{0,4},{4,8},{8,12},{1,5},{5,9},{9,13},{2,6},{6,10},{10,14},{3,7},{... | collective-permute-start | bytes 196616 | tf_op jit(solution)/shard_map/ppermute | solution.py:19
  26.9 98.5 %reduce-scatter.2.cloned.1.call-start = ((), (), s32[]{:S(2)}) async-start(), calls=%async_computation.1 | async-start | bytes 196608 | tf_op jit(solution)/shard_map/reduce_scatter | solution.py:116
  27.4 0.9 copy-start.1
  30.5 2.9 %collective-permute-start.2 = (f32[1,4,32,8]{3,2,1,0:T(8,128)S(1)}, f32[1,4,32,8]{3,2,1,0:T(8,128)S(1)}, u32[]{:S(2)}, u32[]{:S(2)}) collective-permute-start(f32[1,4,32,8]{3,2,1,0:T(8,128)S(1)} %get-tuple-element.96), channel_id=1, source_target_pairs={{0,1},{2,3},{4,5},{6,7},{8,9},{10,11},{12,13},{14,15},{16,17},{18,... | collective-permute-start | bytes 12296 | tf_op jit(solution)/shard_map/ppermute | solution.py:19
  32.0 3.1 %collective-permute-start.3 = (f32[1,4,32,8]{3,2,1,0:T(8,128)S(1)}, f32[1,4,32,8]{3,2,1,0:T(8,128)S(1)}, u32[]{:S(2)}, u32[]{:S(2)}) collective-permute-start(f32[1,4,32,8]{3,2,1,0:T(8,128)S(1)} %get-tuple-element.97), channel_id=1, source_target_pairs={{1,0},{3,2},{5,4},{7,6},{9,8},{11,10},{13,12},{15,14},{17,16},{19,... | collective-permute-start | bytes 12296 | tf_op jit(solution)/shard_map/ppermute | solution.py:21
  52.1 0.8 copy-start.13
  52.1 0.8 copy-start.11
  52.2 0.8 copy-start.6
  52.2 0.8 copy-start.7
  52.2 0.8 copy-start.8
  52.2 0.8 copy-start.9
  52.2 0.8 copy-start.5
  52.2 0.8 copy-start.3
  52.2 0.8 copy-start.4
  53.5 4.9 %copy-start.27 = (f32[16,512]{1,0:T(8,128)S(1)}, f32[16,512]{1,0:T(8,128)}, u32[]{:S(2)}) copy-start(f32[16,512]{1,0:T(8,128)} %get-tuple-element.3) | copy-start | bytes 98308
  53.6 11.3 %collective-permute-start.4 = (f32[1,4,8,512]{3,2,1,0:T(8,128)S(1)}, f32[1,4,8,512]{3,2,1,0:T(8,128)S(1)}, u32[]{:S(2)}, u32[]{:S(2)}) collective-permute-start(f32[1,4,8,512]{3,2,1,0:T(8,128)S(1)} %get-tuple-element.193), channel_id=1, source_target_pairs={{0,4},{4,8},{8,12},{1,5},{5,9},{9,13},{2,6},{6,10},{10,14},{3,7},{... | collective-permute-start | bytes 196616 | tf_op jit(solution)/shard_map/ppermute | solution.py:19
  57.0 7.9 %collective-permute-start.5 = (f32[1,4,8,512]{3,2,1,0:T(8,128)S(1)}, f32[1,4,8,512]{3,2,1,0:T(8,128)S(1)}, u32[]{:S(2)}, u32[]{:S(2)}) collective-permute-start(f32[1,4,8,512]{3,2,1,0:T(8,128)S(1)} %get-tuple-element.194), channel_id=1, source_target_pairs={{4,0},{8,4},{12,8},{5,1},{9,5},{13,9},{6,2},{10,6},{14,10},{7,3},{... | collective-permute-start | bytes 196616 | tf_op jit(solution)/shard_map/ppermute | solution.py:21
  64.9 2.8 %collective-permute-start.6 = (f32[1,4,32,8]{3,2,1,0:T(8,128)S(1)}, f32[1,4,32,8]{3,2,1,0:T(8,128)S(1)}, u32[]{:S(2)}, u32[]{:S(2)}) collective-permute-start(f32[1,4,32,8]{3,2,1,0:T(8,128)S(1)} %get-tuple-element.94), channel_id=1, source_target_pairs={{0,1},{2,3},{4,5},{6,7},{8,9},{10,11},{12,13},{14,15},{16,17},{18,... | collective-permute-start | bytes 12296 | tf_op jit(solution)/shard_map/ppermute | solution.py:19
  66.2 3.1 %collective-permute-start.7 = (f32[1,4,32,8]{3,2,1,0:T(8,128)S(1)}, f32[1,4,32,8]{3,2,1,0:T(8,128)S(1)}, u32[]{:S(2)}, u32[]{:S(2)}) collective-permute-start(f32[1,4,32,8]{3,2,1,0:T(8,128)S(1)} %get-tuple-element.95), channel_id=1, source_target_pairs={{1,0},{3,2},{5,4},{7,6},{9,8},{11,10},{13,12},{15,14},{17,16},{19,... | collective-permute-start | bytes 12296 | tf_op jit(solution)/shard_map/ppermute | solution.py:21
  75.1 6.4 %collective-permute-start.8 = (f32[1,4,8,512]{3,2,1,0:T(8,128)S(1)}, f32[1,4,8,512]{3,2,1,0:T(8,128)S(1)}, u32[]{:S(2)}, u32[]{:S(2)}) collective-permute-start(f32[1,4,8,512]{3,2,1,0:T(8,128)S(1)} %get-tuple-element.187), channel_id=1, source_target_pairs={{0,4},{4,8},{8,12},{1,5},{5,9},{9,13},{2,6},{6,10},{10,14},{3,7},{... | collective-permute-start | bytes 196616 | tf_op jit(solution)/shard_map/ppermute | solution.py:19
  79.7 6.2 %collective-permute-start.9 = (f32[1,4,8,512]{3,2,1,0:T(8,128)S(1)}, f32[1,4,8,512]{3,2,1,0:T(8,128)S(1)}, u32[]{:S(2)}, u32[]{:S(2)}) collective-permute-start(f32[1,4,8,512]{3,2,1,0:T(8,128)S(1)} %get-tuple-element.188), channel_id=1, source_target_pairs={{4,0},{8,4},{12,8},{5,1},{9,5},{13,9},{6,2},{10,6},{14,10},{7,3},{... | collective-permute-start | bytes 196616 | tf_op jit(solution)/shard_map/ppermute | solution.py:21
  85.9 2.8 %collective-permute-start.10 = (f32[1,4,32,8]{3,2,1,0:T(8,128)S(1)}, f32[1,4,32,8]{3,2,1,0:T(8,128)S(1)}, u32[]{:S(2)}, u32[]{:S(2)}) collective-permute-start(f32[1,4,32,8]{3,2,1,0:T(8,128)S(1)} %get-tuple-element.92), channel_id=1, source_target_pairs={{0,1},{2,3},{4,5},{6,7},{8,9},{10,11},{12,13},{14,15},{16,17},{18,... | collective-permute-start | bytes 12296 | tf_op jit(solution)/shard_map/ppermute | solution.py:19
  87.2 3.1 %collective-permute-start.11 = (f32[1,4,32,8]{3,2,1,0:T(8,128)S(1)}, f32[1,4,32,8]{3,2,1,0:T(8,128)S(1)}, u32[]{:S(2)}, u32[]{:S(2)}) collective-permute-start(f32[1,4,32,8]{3,2,1,0:T(8,128)S(1)} %get-tuple-element.93), channel_id=1, source_target_pairs={{1,0},{3,2},{5,4},{7,6},{9,8},{11,10},{13,12},{15,14},{17,16},{19,... | collective-permute-start | bytes 12296 | tf_op jit(solution)/shard_map/ppermute | solution.py:21
  96.1 5.3 %collective-permute-start.12 = (f32[1,4,8,512]{3,2,1,0:T(8,128)S(1)}, f32[1,4,8,512]{3,2,1,0:T(8,128)S(1)}, u32[]{:S(2)}, u32[]{:S(2)}) collective-permute-start(f32[1,4,8,512]{3,2,1,0:T(8,128)S(1)} %get-tuple-element.181), channel_id=1, source_target_pairs={{0,4},{4,8},{8,12},{1,5},{5,9},{9,13},{2,6},{6,10},{10,14},{3,7},{... | collective-permute-start | bytes 196616 | tf_op jit(solution)/shard_map/ppermute | solution.py:19
  99.5 6.2 %collective-permute-start.13 = (f32[1,4,8,512]{3,2,1,0:T(8,128)S(1)}, f32[1,4,8,512]{3,2,1,0:T(8,128)S(1)}, u32[]{:S(2)}, u32[]{:S(2)}) collective-permute-start(f32[1,4,8,512]{3,2,1,0:T(8,128)S(1)} %get-tuple-element.182), channel_id=1, source_target_pairs={{4,0},{8,4},{12,8},{5,1},{9,5},{13,9},{6,2},{10,6},{14,10},{7,3},{... | collective-permute-start | bytes 196616 | tf_op jit(solution)/shard_map/ppermute | solution.py:21
  105.7 2.6 %collective-permute-start.14 = (f32[1,4,32,8]{3,2,1,0:T(8,128)S(1)}, f32[1,4,32,8]{3,2,1,0:T(8,128)S(1)}, u32[]{:S(2)}, u32[]{:S(2)}) collective-permute-start(f32[1,4,32,8]{3,2,1,0:T(8,128)S(1)} %get-tuple-element.90), channel_id=1, source_target_pairs={{0,1},{2,3},{4,5},{6,7},{8,9},{10,11},{12,13},{14,15},{16,17},{18,... | collective-permute-start | bytes 12296 | tf_op jit(solution)/shard_map/ppermute | solution.py:19
  107.0 3.1 %collective-permute-start.15 = (f32[1,4,32,8]{3,2,1,0:T(8,128)S(1)}, f32[1,4,32,8]{3,2,1,0:T(8,128)S(1)}, u32[]{:S(2)}, u32[]{:S(2)}) collective-permute-start(f32[1,4,32,8]{3,2,1,0:T(8,128)S(1)} %get-tuple-element.91), channel_id=1, source_target_pairs={{1,0},{3,2},{5,4},{7,6},{9,8},{11,10},{13,12},{15,14},{17,16},{19,... | collective-permute-start | bytes 12296 | tf_op jit(solution)/shard_map/ppermute | solution.py:21
  (15 other events, 11.7 us)
Sparse Core Ops, SparseCore 0:
  27.0 22.4 all-reduce.2
  116.7 8.5 reduce-scatter.1
where the time goes:
time: 133 us; the launch traced here: 132 us
  starting transfers between devices  33.2 us (25%)
  waiting for transfers between devices  32.2 us (24%)
  between operations  26.7 us (20%)
  other arithmetic  26.5 us (20%)
  local copies, waits for them, and re-layouts  7.93 us (6%)
  matrix products  5.61 us (4%)
    ppermute x8, starting transfers between devices, padded_2(): lax.ppermute(tail, axis, [(i, (i + 1) % count) for i in range(ends)])  22.2 us
    ppermute x8, waiting for transfers between devices, padded_2(): lax.ppermute(head, axis, [((i + 1) % count, i) for i in range(ends)])  15.3 us
    mul x28, other arithmetic, propagate(): (2.0 * stencil(current) - trim_edges(previous, 1)) * trim_edges(inside, o...  14.8 us
    ppermute x8, starting transfers between devices, padded_2(): lax.ppermute(head, axis, [((i + 1) % count, i) for i in range(ends)])  10.9 us
    reduce_scatter x1, waiting for transfers between devices, body(): lax.psum_scatter(jnp.stack(images), 'freq', scatter_dimension=0, tiled=True)  8.7 us
    psum x1, waiting for transfers between devices, spread(): return lax.psum(kept, axis)  7.36 us
    slice x29, other arithmetic, combine(): term[:, 1]  5.18 us
    dot_general x4, matrix products, body(): jnp.dot(selected, weights, precision=highest, preferred_element_type=jnp....  4.92 us
  transfers between devices with their start and end apart: 18, of which 10 were waited for; matrix products, arithmetic and copies ran while one was open for 12% of the time, Pallas kernels for 0%

commit v1 on v0

--- a/solution.py
+++ b/solution.py
@@ -27,7 +27,7 @@
 
 def spread(value, axis, source):
     kept = jnp.where(lax.axis_index(axis) == source, value, 0).astype(value.dtype)
-    return lax.psum(kept, axis)
+    return jnp.sum(lax.all_gather(kept, axis), axis=0)
 
 
 def stencil(padded):

time: 133 us -> 142 us (1.068)
  blocking collectives: 0 us -> 18.3 us
  other arithmetic: 26.5 us -> 23.4 us
  waiting for transfers between devices: 32.2 us -> 29.3 us
  local copies, waits for them, and re-layouts: 7.93 us -> 6.27 us
    all_gather x0 -> x4, blocking collectives: none -> 18.3 us  [spread(): return jnp.sum(lax.all_gather(kept, axis), axis=0)]
    psum x1 -> x0, waiting for transfers between devices: 7.36 us -> none  [spread(): return lax.psum(kept, axis)]
    ppermute x8, waiting for transfers between devices: 15.3 us -> 19.5 us  [padded_2(): lax.ppermute(head, axis, [((i + 1) % count, i) for i in range(ends)])]
    slice x29, other arithmetic: 5.18 us -> 2.67 us  [combine(): term[:, 1]]
    unnamed x128 -> x80, local copies, waits for them, and re-layouts: 3.4 us -> 1.83 us
  transfers between devices with their start and end apart: 18 -> 17, of which waited for: 10 -> 11; matrix products, arithmetic and copies ran while one was open for 12% -> 6% of each run, Pallas kernels for 0% -> 0%
where the time goes in v1:
time: 142 us; the launch traced here: 141 us
  starting transfers between devices  32.4 us (23%)
  waiting for transfers between devices  29.3 us (21%)
  between operations  26.6 us (19%)
  other arithmetic  23.4 us (16%)
  blocking collectives  18.3 us (13%)
  local copies, waits for them, and re-layouts  6.27 us (4%)
  matrix products  4.86 us (3%)
    ppermute x8, starting transfers between devices, padded_2(): lax.ppermute(tail, axis, [(i, (i + 1) % count) for i in range(ends)])  21.6 us
    ppermute x8, waiting for transfers between devices, padded_2(): lax.ppermute(head, axis, [((i + 1) % count, i) for i in range(ends)])  19.5 us
    all_gather x4, blocking collectives, spread(): return jnp.sum(lax.all_gather(kept, axis), axis=0)  18.3 us
    mul x28, other arithmetic, propagate(): (2.0 * stencil(current) - trim_edges(previous, 1)) * trim_edges(inside, o...  14.7 us
    ppermute x8, starting transfers between devices, padded_2(): lax.ppermute(head, axis, [((i + 1) % count, i) for i in range(ends)])  10.7 us
    reduce_scatter x1, waiting for transfers between devices, body(): lax.psum_scatter(jnp.stack(images), 'freq', scatter_dimension=0, tiled=True)  8.73 us
    dot_general x4, matrix products, body(): jnp.dot(selected, weights, precision=highest, preferred_element_type=jnp....  4.17 us
  transfers between devices with their start and end apart: 17, of which 11 were waited for; matrix products, arithmetic and copies ran while one was open for 6% of the time, Pallas kernels for 0%

profile of v1, /device:TPU:0, one launch (start us, length us, event | category | flops | bytes accessed | tf_op | source)
XLA Modules:
  0.0 141.2 jit_solution(16068159029462983289)
XLA Ops:
  8.2 5.0 %collective-permute-start = (f32[1,4,8,512]{3,2,1,0:T(8,128)S(1)}, f32[1,4,8,512]{3,2,1,0:T(8,128)S(1)}, u32[]{:S(2)}, u32[]{:S(2)}) collective-permute-start(f32[1,4,8,512]{3,2,1,0:T(8,128)S(1)} %get-tuple-element.204), channel_id=1, source_target_pairs={{0,4},{4,8},{8,12},{1,5},{5,9},{9,13},{2,6},{6,10},{10,14},{3,7},{... | collective-permute-start | bytes 196616 | tf_op jit(solution)/shard_map/ppermute | solution.py:19
  13.1 1.3 collective-permute-start.1
  27.7 4.6 %all_gather.19 = f32[2,16,512]{2,1,0:T(8,128)S(1)} all-gather(f32[1,16,512]{2,1,0:T(8,128)S(1)} %get-tuple-element.175), channel_id=1, replica_groups=mesh['shots'=2,'lat'=4,'freq'=2,'sub'=2] {'freq'}, dimensions={0}, use_global_device_ids=true | all-gather | bytes 98304 | tf_op jit(solution)/shard_map/all_gather | solution.py:30
  33.7 1.0 convolution_bitcast_fusion
  35.3 4.6 %all_gather.18 = f32[2,16,512]{2,1,0:T(8,128)S(1)} all-gather(f32[1,16,512]{2,1,0:T(8,128)S(1)} %get-tuple-element.176), channel_id=1, replica_groups=mesh['shots'=2,'lat'=4,'freq'=2,'sub'=2] {'freq'}, dimensions={0}, use_global_device_ids=true | all-gather | bytes 98304 | tf_op jit(solution)/shard_map/all_gather | solution.py:30
  39.9 1.0 convolution_bitcast_fusion.1
  41.4 4.6 %all_gather.17 = f32[2,16,512]{2,1,0:T(8,128)S(1)} all-gather(f32[1,16,512]{2,1,0:T(8,128)S(1)} %get-tuple-element.174), channel_id=1, replica_groups=mesh['shots'=2,'lat'=4,'freq'=2,'sub'=2] {'freq'}, dimensions={0}, use_global_device_ids=true | all-gather | bytes 98304 | tf_op jit(solution)/shard_map/all_gather | solution.py:30
  46.0 1.0 convolution_bitcast_fusion.2
  47.6 4.6 %all_gather.16 = f32[2,16,512]{2,1,0:T(8,128)S(1)} all-gather(f32[1,16,512]{2,1,0:T(8,128)S(1)} %get-tuple-element.173), channel_id=1, replica_groups=mesh['shots'=2,'lat'=4,'freq'=2,'sub'=2] {'freq'}, dimensions={0}, use_global_device_ids=true | all-gather | bytes 98304 | tf_op jit(solution)/shard_map/all_gather | solution.py:30
  52.1 1.0 convolution_bitcast_fusion.3
  54.1 1.3 collective-permute-start.2
  55.4 1.5 %collective-permute-start.3 = (f32[1,4,32,8]{3,2,1,0:T(8,128)S(1)}, f32[1,4,32,8]{3,2,1,0:T(8,128)S(1)}, u32[]{:S(2)}, u32[]{:S(2)}) collective-permute-start(f32[1,4,32,8]{3,2,1,0:T(8,128)S(1)} %get-tuple-element.93), channel_id=1, source_target_pairs={{1,0},{3,2},{5,4},{7,6},{9,8},{11,10},{13,12},{15,14},{17,16},{19,... | collective-permute-start | bytes 12296 | tf_op jit(solution)/shard_map/ppermute | solution.py:21
  57.2 1.4 collective-permute-done.3
  64.1 4.5 %collective-permute-start.4 = (f32[1,4,8,512]{3,2,1,0:T(8,128)S(1)}, f32[1,4,8,512]{3,2,1,0:T(8,128)S(1)}, u32[]{:S(2)}, u32[]{:S(2)}) collective-permute-start(f32[1,4,8,512]{3,2,1,0:T(8,128)S(1)} %get-tuple-element.193), channel_id=1, source_target_pairs={{0,4},{4,8},{8,12},{1,5},{5,9},{9,13},{2,6},{6,10},{10,14},{3,7},{... | collective-permute-start | bytes 196616 | tf_op jit(solution)/shard_map/ppermute | solution.py:19
  68.6 1.3 collective-permute-start.5
  70.5 4.3 %collective-permute-done.5 = f32[1,4,8,512]{3,2,1,0:T(8,128)S(1)} collective-permute-done((f32[1,4,8,512]{3,2,1,0:T(8,128)S(1)}, f32[1,4,8,512]{3,2,1,0:T(8,128)S(1)}, u32[]{:S(2)}, u32[]{:S(2)}) %collective-permute-start.5) | collective-permute-done | bytes 65568 | tf_op jit(solution)/shard_map/ppermute | solution.py:21
  74.9 1.3 collective-permute-start.6
  76.2 1.3 collective-permute-start.7
  77.5 1.8 %collective-permute-done.7 = f32[1,4,32,8]{3,2,1,0:T(8,128)S(1)} collective-permute-done((f32[1,4,32,8]{3,2,1,0:T(8,128)S(1)}, f32[1,4,32,8]{3,2,1,0:T(8,128)S(1)}, u32[]{:S(2)}, u32[]{:S(2)}) %collective-permute-start.7) | collective-permute-done | bytes 4128 | tf_op jit(solution)/shard_map/ppermute | solution.py:21
  85.1 3.5 %collective-permute-start.8 = (f32[1,4,8,512]{3,2,1,0:T(8,128)S(1)}, f32[1,4,8,512]{3,2,1,0:T(8,128)S(1)}, u32[]{:S(2)}, u32[]{:S(2)}) collective-permute-start(f32[1,4,8,512]{3,2,1,0:T(8,128)S(1)} %get-tuple-element.187), channel_id=1, source_target_pairs={{0,4},{4,8},{8,12},{1,5},{5,9},{9,13},{2,6},{6,10},{10,14},{3,7},{... | collective-permute-start | bytes 196616 | tf_op jit(solution)/shard_map/ppermute | solution.py:19
  88.6 1.3 collective-permute-start.9
  90.4 4.3 %collective-permute-done.9 = f32[1,4,8,512]{3,2,1,0:T(8,128)S(1)} collective-permute-done((f32[1,4,8,512]{3,2,1,0:T(8,128)S(1)}, f32[1,4,8,512]{3,2,1,0:T(8,128)S(1)}, u32[]{:S(2)}, u32[]{:S(2)}) %collective-permute-start.9) | collective-permute-done | bytes 65568 | tf_op jit(solution)/shard_map/ppermute | solution.py:21
  94.8 1.3 collective-permute-start.10
  96.1 1.5 %collective-permute-start.11 = (f32[1,4,32,8]{3,2,1,0:T(8,128)S(1)}, f32[1,4,32,8]{3,2,1,0:T(8,128)S(1)}, u32[]{:S(2)}, u32[]{:S(2)}) collective-permute-start(f32[1,4,32,8]{3,2,1,0:T(8,128)S(1)} %get-tuple-element.89), channel_id=1, source_target_pairs={{1,0},{3,2},{5,4},{7,6},{9,8},{11,10},{13,12},{15,14},{17,16},{19,... | collective-permute-start | bytes 12296 | tf_op jit(solution)/shard_map/ppermute | solution.py:21
  97.7 1.6 %collective-permute-done.11 = f32[1,4,32,8]{3,2,1,0:T(8,128)S(1)} collective-permute-done((f32[1,4,32,8]{3,2,1,0:T(8,128)S(1)}, f32[1,4,32,8]{3,2,1,0:T(8,128)S(1)}, u32[]{:S(2)}, u32[]{:S(2)}) %collective-permute-start.11) | collective-permute-done | bytes 4128 | tf_op jit(solution)/shard_map/ppermute | solution.py:21
  105.0 3.5 %collective-permute-start.12 = (f32[1,4,8,512]{3,2,1,0:T(8,128)S(1)}, f32[1,4,8,512]{3,2,1,0:T(8,128)S(1)}, u32[]{:S(2)}, u32[]{:S(2)}) collective-permute-start(f32[1,4,8,512]{3,2,1,0:T(8,128)S(1)} %get-tuple-element.181), channel_id=1, source_target_pairs={{0,4},{4,8},{8,12},{1,5},{5,9},{9,13},{2,6},{6,10},{10,14},{3,7},{... | collective-permute-start | bytes 196616 | tf_op jit(solution)/shard_map/ppermute | solution.py:19
  108.5 1.3 collective-permute-start.13
  110.4 4.3 %collective-permute-done.13 = f32[1,4,8,512]{3,2,1,0:T(8,128)S(1)} collective-permute-done((f32[1,4,8,512]{3,2,1,0:T(8,128)S(1)}, f32[1,4,8,512]{3,2,1,0:T(8,128)S(1)}, u32[]{:S(2)}, u32[]{:S(2)}) %collective-permute-start.13) | collective-permute-done | bytes 65568 | tf_op jit(solution)/shard_map/ppermute | solution.py:21
  114.7 1.3 collective-permute-start.14
  116.0 1.3 collective-permute-start.15
  117.3 1.8 %collective-permute-done.15 = f32[1,4,32,8]{3,2,1,0:T(8,128)S(1)} collective-permute-done((f32[1,4,32,8]{3,2,1,0:T(8,128)S(1)}, f32[1,4,32,8]{3,2,1,0:T(8,128)S(1)}, u32[]{:S(2)}, u32[]{:S(2)}) %collective-permute-start.15) | collective-permute-done | bytes 4128 | tf_op jit(solution)/shard_map/ppermute | solution.py:21
  125.6 8.7 %reduce-scatter.2.cloned.1.call-done = f32[2,16,512]{2,1,0:T(8,128)} async-done(((f32[4,16,512]{2,1,0:T(8,128)}), f32[2,16,512]{2,1,0:T(8,128)}) %reduce-scatter.2.cloned.1.call-update) | async-done | bytes 65552 | tf_op jit(solution)/shard_map/reduce_scatter | solution.py:116
  (218 shorter events, 31.5 us)
Async XLA Ops:
  7.2 25.8 %copy-start = (f32[32,32,9,2]{1,3,2,0:T(2,128)S(1)}, f32[32,32,9,2]{1,3,2,0:T(2,128)}, u32[]{:S(2)}) copy-start(f32[32,32,9,2]{1,3,2,0:T(2,128)} %param.7) | copy-start | bytes 221188
  7.2 127.1 %reduce-scatter.2.cloned.1.call-start = ((), (), s32[]{:S(2)}) async-start(), calls=%async_computation.1 | async-start | bytes 196608 | tf_op jit(solution)/shard_map/reduce_scatter | solution.py:116
  8.1 6.3 %copy-start.4 = (s32[4]{0:T(128)S(1)}, s32[4]{0:T(128)}, u32[]{:S(2)}) copy-start(s32[4]{0:T(128)} %param.9) | copy-start | bytes 52
  8.2 45.8 %collective-permute-start = (f32[1,4,8,512]{3,2,1,0:T(8,128)S(1)}, f32[1,4,8,512]{3,2,1,0:T(8,128)S(1)}, u32[]{:S(2)}, u32[]{:S(2)}) collective-permute-start(f32[1,4,8,512]{3,2,1,0:T(8,128)S(1)} %get-tuple-element.204), channel_id=1, source_target_pairs={{0,4},{4,8},{8,12},{1,5},{5,9},{9,13},{2,6},{6,10},{10,14},{3,7},{... | collective-permute-start | bytes 196616 | tf_op jit(solution)/shard_map/ppermute | solution.py:19
  13.1 40.9 %collective-permute-start.1 = (f32[1,4,8,512]{3,2,1,0:T(8,128)S(1)}, f32[1,4,8,512]{3,2,1,0:T(8,128)S(1)}, u32[]{:S(2)}, u32[]{:S(2)}) collective-permute-start(f32[1,4,8,512]{3,2,1,0:T(8,128)S(1)} %get-tuple-element.203), channel_id=1, source_target_pairs={{4,0},{8,4},{12,8},{5,1},{9,5},{13,9},{6,2},{10,6},{14,10},{7,3},{... | collective-permute-start | bytes 196616 | tf_op jit(solution)/shard_map/ppermute | solution.py:21
  25.9 0.9 copy-start.1
  26.8 0.9 copy-start.3
  54.1 3.0 %collective-permute-start.2 = (f32[1,4,32,8]{3,2,1,0:T(8,128)S(1)}, f32[1,4,32,8]{3,2,1,0:T(8,128)S(1)}, u32[]{:S(2)}, u32[]{:S(2)}) collective-permute-start(f32[1,4,32,8]{3,2,1,0:T(8,128)S(1)} %get-tuple-element.92), channel_id=1, source_target_pairs={{0,1},{2,3},{4,5},{6,7},{8,9},{10,11},{12,13},{14,15},{16,17},{18,... | collective-permute-start | bytes 12296 | tf_op jit(solution)/shard_map/ppermute | solution.py:19
  55.4 3.1 %collective-permute-start.3 = (f32[1,4,32,8]{3,2,1,0:T(8,128)S(1)}, f32[1,4,32,8]{3,2,1,0:T(8,128)S(1)}, u32[]{:S(2)}, u32[]{:S(2)}) collective-permute-start(f32[1,4,32,8]{3,2,1,0:T(8,128)S(1)} %get-tuple-element.93), channel_id=1, source_target_pairs={{1,0},{3,2},{5,4},{7,6},{9,8},{11,10},{13,12},{15,14},{17,16},{19,... | collective-permute-start | bytes 12296 | tf_op jit(solution)/shard_map/ppermute | solution.py:21
  64.1 6.4 %collective-permute-start.4 = (f32[1,4,8,512]{3,2,1,0:T(8,128)S(1)}, f32[1,4,8,512]{3,2,1,0:T(8,128)S(1)}, u32[]{:S(2)}, u32[]{:S(2)}) collective-permute-start(f32[1,4,8,512]{3,2,1,0:T(8,128)S(1)} %get-tuple-element.193), channel_id=1, source_target_pairs={{0,4},{4,8},{8,12},{1,5},{5,9},{9,13},{2,6},{6,10},{10,14},{3,7},{... | collective-permute-start | bytes 196616 | tf_op jit(solution)/shard_map/ppermute | solution.py:19
  68.6 6.2 %collective-permute-start.5 = (f32[1,4,8,512]{3,2,1,0:T(8,128)S(1)}, f32[1,4,8,512]{3,2,1,0:T(8,128)S(1)}, u32[]{:S(2)}, u32[]{:S(2)}) collective-permute-start(f32[1,4,8,512]{3,2,1,0:T(8,128)S(1)} %get-tuple-element.194), channel_id=1, source_target_pairs={{4,0},{8,4},{12,8},{5,1},{9,5},{13,9},{6,2},{10,6},{14,10},{7,3},{... | collective-permute-start | bytes 196616 | tf_op jit(solution)/shard_map/ppermute | solution.py:21
  74.9 2.6 %collective-permute-start.6 = (f32[1,4,32,8]{3,2,1,0:T(8,128)S(1)}, f32[1,4,32,8]{3,2,1,0:T(8,128)S(1)}, u32[]{:S(2)}, u32[]{:S(2)}) collective-permute-start(f32[1,4,32,8]{3,2,1,0:T(8,128)S(1)} %get-tuple-element.90), channel_id=1, source_target_pairs={{0,1},{2,3},{4,5},{6,7},{8,9},{10,11},{12,13},{14,15},{16,17},{18,... | collective-permute-start | bytes 12296 | tf_op jit(solution)/shard_map/ppermute | solution.py:19
  76.2 3.1 %collective-permute-start.7 = (f32[1,4,32,8]{3,2,1,0:T(8,128)S(1)}, f32[1,4,32,8]{3,2,1,0:T(8,128)S(1)}, u32[]{:S(2)}, u32[]{:S(2)}) collective-permute-start(f32[1,4,32,8]{3,2,1,0:T(8,128)S(1)} %get-tuple-element.91), channel_id=1, source_target_pairs={{1,0},{3,2},{5,4},{7,6},{9,8},{11,10},{13,12},{15,14},{17,16},{19,... | collective-permute-start | bytes 12296 | tf_op jit(solution)/shard_map/ppermute | solution.py:21
  85.1 5.4 %collective-permute-start.8 = (f32[1,4,8,512]{3,2,1,0:T(8,128)S(1)}, f32[1,4,8,512]{3,2,1,0:T(8,128)S(1)}, u32[]{:S(2)}, u32[]{:S(2)}) collective-permute-start(f32[1,4,8,512]{3,2,1,0:T(8,128)S(1)} %get-tuple-element.187), channel_id=1, source_target_pairs={{0,4},{4,8},{8,12},{1,5},{5,9},{9,13},{2,6},{6,10},{10,14},{3,7},{... | collective-permute-start | bytes 196616 | tf_op jit(solution)/shard_map/ppermute | solution.py:19
  88.6 6.2 %collective-permute-start.9 = (f32[1,4,8,512]{3,2,1,0:T(8,128)S(1)}, f32[1,4,8,512]{3,2,1,0:T(8,128)S(1)}, u32[]{:S(2)}, u32[]{:S(2)}) collective-permute-start(f32[1,4,8,512]{3,2,1,0:T(8,128)S(1)} %get-tuple-element.188), channel_id=1, source_target_pairs={{4,0},{8,4},{12,8},{5,1},{9,5},{13,9},{6,2},{10,6},{14,10},{7,3},{... | collective-permute-start | bytes 196616 | tf_op jit(solution)/shard_map/ppermute | solution.py:21
  94.8 2.8 %collective-permute-start.10 = (f32[1,4,32,8]{3,2,1,0:T(8,128)S(1)}, f32[1,4,32,8]{3,2,1,0:T(8,128)S(1)}, u32[]{:S(2)}, u32[]{:S(2)}) collective-permute-start(f32[1,4,32,8]{3,2,1,0:T(8,128)S(1)} %get-tuple-element.88), channel_id=1, source_target_pairs={{0,1},{2,3},{4,5},{6,7},{8,9},{10,11},{12,13},{14,15},{16,17},{18,... | collective-permute-start | bytes 12296 | tf_op jit(solution)/shard_map/ppermute | solution.py:19
  96.1 3.1 %collective-permute-start.11 = (f32[1,4,32,8]{3,2,1,0:T(8,128)S(1)}, f32[1,4,32,8]{3,2,1,0:T(8,128)S(1)}, u32[]{:S(2)}, u32[]{:S(2)}) collective-permute-start(f32[1,4,32,8]{3,2,1,0:T(8,128)S(1)} %get-tuple-element.89), channel_id=1, source_target_pairs={{1,0},{3,2},{5,4},{7,6},{9,8},{11,10},{13,12},{15,14},{17,16},{19,... | collective-permute-start | bytes 12296 | tf_op jit(solution)/shard_map/ppermute | solution.py:21
  105.0 5.4 %collective-permute-start.12 = (f32[1,4,8,512]{3,2,1,0:T(8,128)S(1)}, f32[1,4,8,512]{3,2,1,0:T(8,128)S(1)}, u32[]{:S(2)}, u32[]{:S(2)}) collective-permute-start(f32[1,4,8,512]{3,2,1,0:T(8,128)S(1)} %get-tuple-element.181), channel_id=1, source_target_pairs={{0,4},{4,8},{8,12},{1,5},{5,9},{9,13},{2,6},{6,10},{10,14},{3,7},{... | collective-permute-start | bytes 196616 | tf_op jit(solution)/shard_map/ppermute | solution.py:19
  108.5 6.2 %collective-permute-start.13 = (f32[1,4,8,512]{3,2,1,0:T(8,128)S(1)}, f32[1,4,8,512]{3,2,1,0:T(8,128)S(1)}, u32[]{:S(2)}, u32[]{:S(2)}) collective-permute-start(f32[1,4,8,512]{3,2,1,0:T(8,128)S(1)} %get-tuple-element.182), channel_id=1, source_target_pairs={{4,0},{8,4},{12,8},{5,1},{9,5},{13,9},{6,2},{10,6},{14,10},{7,3},{... | collective-permute-start | bytes 196616 | tf_op jit(solution)/shard_map/ppermute | solution.py:21
  114.7 2.6 %collective-permute-start.14 = (f32[1,4,32,8]{3,2,1,0:T(8,128)S(1)}, f32[1,4,32,8]{3,2,1,0:T(8,128)S(1)}, u32[]{:S(2)}, u32[]{:S(2)}) collective-permute-start(f32[1,4,32,8]{3,2,1,0:T(8,128)S(1)} %get-tuple-element.86), channel_id=1, source_target_pairs={{0,1},{2,3},{4,5},{6,7},{8,9},{10,11},{12,13},{14,15},{16,17},{18,... | collective-permute-start | bytes 12296 | tf_op jit(solution)/shard_map/ppermute | solution.py:19
  116.0 3.1 %collective-permute-start.15 = (f32[1,4,32,8]{3,2,1,0:T(8,128)S(1)}, f32[1,4,32,8]{3,2,1,0:T(8,128)S(1)}, u32[]{:S(2)}, u32[]{:S(2)}) collective-permute-start(f32[1,4,32,8]{3,2,1,0:T(8,128)S(1)} %get-tuple-element.87), channel_id=1, source_target_pairs={{1,0},{3,2},{5,4},{7,6},{9,8},{11,10},{13,12},{15,14},{17,16},{19,... | collective-permute-start | bytes 12296 | tf_op jit(solution)/shard_map/ppermute | solution.py:21
  124.9 0.7 copy-start.2
Sparse Core Ops, SparseCore 0:
  125.7 8.5 reduce-scatter.1
